TPU v7x, 128 devices: a whole 4x4x4 slice. The times are simulated.
128 devices in a mesh: req: 32 (over y, z, core), kvh: 4 (over x).
Axes of the slice: x: 4, y: 4, z: 4, core: 2. Of those that a mesh axis runs over, the one named last changes fastest.
Arguments:
- queries: bfloat16 [2048, 4, 8, 128], P('req', 'kvh')
- key_cache: bfloat16 [5120, 4, 128, 128], P('req', 'kvh')
- value_cache: bfloat16 [5120, 4, 128, 128], P('req', 'kvh'), may hold values from -24 to 24
- lengths: int32 [2048], P('req'), may hold values from 1 to 4096, as said below
- page_table: int32 [2048, 32], P('req'), may hold values from 0 to 159, as said below
- residual_in: bfloat16 [2048, 2048], P(('req', 'kvh')), may hold values from -4 to 4
- w_out: bfloat16 [4096, 2048], P('kvh'), may hold values from -0.09375 to 0.09375
- norm_gain: bfloat16 [2048], replicated, may hold values from 0.099609375 to 1.8984375
- route_logits: float32 [2048, 8], P(('req', 'kvh'))
- routes: int32 [2048, 8], P(('req', 'kvh')), may hold values from 0 to 127, as said below
- w_gate: bfloat16 [128, 2048, 768], P(('req', 'kvh')), may hold values from -0.125 to 0.125
- w_up: bfloat16 [128, 2048, 768], P(('req', 'kvh')), may hold values from -0.125 to 0.125
- w_down: bfloat16 [128, 768, 2048], P(('req', 'kvh')), may hold values from -0.21875 to 0.21875
Outputs:
- layer_out: bfloat16 [2048, 2048], P(('req', 'kvh'))
Inputs may be any that keep to these rules, and one draw needn't show every extreme that they name: `lengths`: every request of a block of 64 has between 1 and 32 pages; some request reaches 4096. `page_table`: local page numbers within the pool of the request's block of 64 requests. Entries 0 to ceil(lengths / 128) - 1 of the requests of one block are all distinct; later entries repeat the request's last used page. `routes`: each token names 8 different experts. Of the 16 tokens of one device, at most 2 name the same expert, and some expert is named by exactly 2 tokens of every device.
All inputs are finite; a program needn't handle non-finite values.
Results may differ from a plain program's by a relative error of at most 0.0054.
Values may be sent and summed in bfloat16 or wider, within the bound.
No kernel may reach another device: no remote copies, remote signals or barrier semaphores. Data moves between devices by JAX's collectives and lax.ppermute only.
A program may use at most 192 MiB of HBM per device.

v0:
```python
import jax
import jax.numpy as jnp
from jax import lax
from jax.sharding import PartitionSpec as P


def swish_gate(gate_part, up_part):
    return gate_part / (1.0 + jnp.exp(-gate_part)) * up_part


def usable_slots(lengths, page_table, pool_pages, page_slots):
    entry_count = page_table.shape[1]
    used_pages = (lengths + page_slots - 1) // page_slots
    columns = jnp.arange(entry_count, dtype=jnp.int32)
    pool_ids = jnp.arange(pool_pages, dtype=jnp.int32)
    matched = (page_table[:, :, None] == pool_ids[None, None, :]) & (
        columns[None, :, None] < used_pages[:, None, None]
    )
    owned_page = jnp.any(matched, axis=1)
    first_pos = jnp.sum(jnp.where(matched, columns[None, :, None] * page_slots, 0), axis=1)
    offsets = jnp.arange(page_slots, dtype=jnp.int32)
    position = first_pos[:, :, None] + offsets[None, None, :]
    usable = owned_page[:, :, None] & (position < lengths[:, None, None])
    return usable.reshape(lengths.shape[0], pool_pages * page_slots)


def earlier_count(pair_routes):
    positions = jnp.arange(pair_routes.shape[0], dtype=jnp.int32)
    same_expert = pair_routes[:, None] == pair_routes[None, :]
    before = positions[None, :] < positions[:, None]
    return jnp.sum(same_expert & before, axis=1)


def local(
    queries,
    key_cache,
    value_cache,
    lengths,
    page_table,
    residual_in,
    w_out,
    norm_gain,
    route_logits,
    routes,
    w_gate,
    w_up,
    w_down,
):
    req_count, single_head, group_count, head_dim = queries.shape
    pool_pages, single_kv, page_slots, key_dim = key_cache.shape
    usable = usable_slots(lengths, page_table, pool_pages, page_slots)
    query_rows = queries.reshape(req_count * group_count, head_dim)
    key_rows = key_cache.reshape(pool_pages * page_slots, head_dim)
    value_rows = value_cache.reshape(pool_pages * page_slots, head_dim)
    scores = jnp.einsum(
        "qd,kd->qk", query_rows, key_rows, preferred_element_type=jnp.float32
    ) * head_dim ** (-0.5)
    scores = scores.reshape(req_count, group_count, pool_pages * page_slots)
    key_mask = usable[:, None, :]
    row_max = jnp.max(jnp.where(key_mask, scores, -jnp.inf), axis=-1, keepdims=True)
    weights = jnp.where(key_mask, jnp.exp(scores - row_max), 0.0)
    denominator = jnp.sum(weights, axis=-1, keepdims=True)
    rounded = weights.astype(jnp.bfloat16).reshape(req_count * group_count, pool_pages * page_slots)
    mixed_values = jnp.dot(rounded, value_rows, preferred_element_type=jnp.float32).reshape(
        req_count, group_count, head_dim
    )
    attended = (
        (mixed_values / denominator).astype(jnp.bfloat16).reshape(req_count, group_count * head_dim)
    )
    stream = residual_in.astype(jnp.float32) + lax.psum_scatter(
        jnp.dot(attended, w_out, preferred_element_type=jnp.float32),
        "kvh",
        scatter_dimension=0,
        tiled=True,
    )
    inverse_rms = lax.rsqrt(jnp.mean(stream * stream, axis=-1, keepdims=True) + 1e-06)
    normed = (stream * inverse_rms * norm_gain.astype(jnp.float32)).astype(jnp.bfloat16)
    logit_max = jnp.max(route_logits, axis=-1, keepdims=True)
    logit_exp = jnp.exp(route_logits - logit_max)
    gate_weights = logit_exp / jnp.sum(logit_exp, axis=-1, keepdims=True)
    expert_count = lax.axis_size("req") * lax.axis_size("kvh")
    token_count, pick_count = routes.shape
    model_width = normed.shape[1]
    slot_depth = max(2, 2 * token_count * pick_count // expert_count)
    pair_routes = routes.reshape(token_count * pick_count)
    pair_slots = earlier_count(pair_routes)
    target = pair_routes * slot_depth + pair_slots
    slot_ids = jnp.arange(expert_count * slot_depth, dtype=jnp.int32)
    chosen = (target[None, :] == slot_ids[:, None]).reshape(
        expert_count * slot_depth, token_count, pick_count
    )
    send_matrix = jnp.any(chosen, axis=-1).astype(jnp.bfloat16)
    outgoing = jnp.dot(send_matrix, normed, preferred_element_type=jnp.float32).astype(jnp.bfloat16)
    outgoing = outgoing.reshape(expert_count, slot_depth, model_width)
    arrived = lax.all_to_all(outgoing, ("req", "kvh"), split_axis=0, concat_axis=0, tiled=True)
    sources, width_slots, arrived_width = arrived.shape
    flat_rows = arrived.reshape(sources * width_slots, arrived_width)
    gate_part = jnp.dot(flat_rows, w_gate[0], preferred_element_type=jnp.float32)
    up_part = jnp.dot(flat_rows, w_up[0], preferred_element_type=jnp.float32)
    hidden = swish_gate(gate_part, up_part).astype(jnp.bfloat16)
    produced = jnp.dot(hidden, w_down[0], preferred_element_type=jnp.float32).astype(jnp.bfloat16)
    returned = lax.all_to_all(
        produced.reshape(sources, width_slots, arrived_width),
        ("req", "kvh"),
        split_axis=0,
        concat_axis=0,
        tiled=True,
    )
    returned = returned.reshape(expert_count * slot_depth, model_width)
    pick_matrix = (target[:, None] == slot_ids[None, :]).astype(jnp.bfloat16)
    picked = jnp.dot(pick_matrix, returned, preferred_element_type=jnp.float32).reshape(
        token_count, pick_count, model_width
    )
    mixture = jnp.sum(gate_weights[:, :, None] * picked, axis=1)
    return (stream + mixture).astype(jnp.bfloat16)


def solution(mesh):
    in_specs = (
        P("req", "kvh", None, None),
        P("req", "kvh", None, None),
        P("req", "kvh", None, None),
        P("req"),
        P("req", None),
        P(("req", "kvh"), None),
        P("kvh", None),
        P(),
        P(("req", "kvh"), None),
        P(("req", "kvh"), None),
        P(("req", "kvh"), None, None),
        P(("req", "kvh"), None, None),
        P(("req", "kvh"), None, None),
    )
    out_specs = P(("req", "kvh"), None)
    return jax.shard_map(local, mesh=mesh, in_specs=in_specs, out_specs=out_specs, check_vma=False)
```

profile of v0, /device:TPU:1, one launch (start us, length us, event | category | flops | bytes accessed | tf_op | source)
XLA Modules:
  0.0 188.0 jit_solution(18326336104326885083)
XLA Ops:
  6.6 0.9 copy.22
  7.5 0.7 and_select_fusion
  8.2 0.1 iota_compare_fusion.4
  8.3 0.7 fusion.19
  9.0 1.0 select_reduce_fusion
  10.1 1.5 add.62
  11.6 1.9 %and.33 = pred[64,160,128]{2,1,0:T(8,128)(4,1)S(1)} broadcast(pred[64,160]{1,0:T(8,128)(4,1)S(1)} %fusion.19), dimensions={0,1} | broadcast | bytes 1320960 | tf_op jit(solution)/shard_map/and | solution.py:23
  13.5 4.4 %fusion.8 = pred[64,20480]{1,0:T(8,128)(4,1)S(1)} fusion(s32[8,8,160,128]{3,2,1,0:T(8,128)S(1)} %bitcast.75, pred[8,8,160,128]{3,2,1,0:T(8,128)(4,1)S(1)} %bitcast.77, s32[64]{0:T(128)S(1)} %copy-done.8, s32[20480]{0:T(1024)S(1)} %iota_bitcast_fusion), kind=kLoop, calls=%fused_computation.10 | loop fusion | flops 3932160 | bytes 7946496 | tf_op jit(solution)/shard_map/and | solution.py:23
  18.0 18.7 %fusion = (f32[512]{0:T(512)S(1)}, f32[512,20480]{1,0:T(8,128)}) fusion(pred[64,20480]{1,0:T(8,128)(4,1)S(1)} %fusion.8, bf16[20480,128]{1,0:T(8,128)(2,1)} %bitcast.76, bf16[64,1,8,128]{3,2,1,0:T(8,128)(2,1)S(1)} %copy-done.4), kind=kOutput, calls=%fused_computation.2 | convolution fusion | flops 2715811328 | bytes 48629760 | tf_op jit(solution)/shard_map/qd,kd->qk/dot_general | solution.py:55
  36.7 19.6 %fusion.1 = f32[512]{0:T(512)S(1)} fusion(f32[512,20480]{1,0:T(8,128)} %get-tuple-element.6, f32[512]{0:T(512)S(1)} %get-tuple-element.5, pred[64,20480]{1,0:T(8,128)(4,1)S(1)} %fusion.8), kind=kLoop, calls=%fused_computation.3 | loop fusion | flops 41942528 | bytes 43257856 | tf_op jit(solution)/shard_map/reduce_sum | solution.py:62
  56.3 0.1 div.40
  56.4 18.6 %fusion.30 = bf16[64,8,128]{2,1,0:T(8,128)(2,1)S(1)} fusion(bf16[20480,128,1]{1,0,2:T(8,128)(2,1)} %bitcast.79, f32[512,20480]{1,0:T(8,128)} %get-tuple-element.6, f32[512]{0:T(512)S(1)} %get-tuple-element.5, pred[64,20480]{1,0:T(8,128)(4,1)} %copy-done.1, f32[64,8]{1,0:T(8,128)S(1)} %div.40), kind=kOutput, calls=%fused_computation.28 | convolution fusion | flops 2726428672 | bytes 48631808 | tf_op jit(solution)/shard_map/dot_general | solution.py:64
  75.1 3.9 %fusion.36 = f32[64,2048]{1,0:T(8,128)} fusion(bf16[1024,2048]{1,0:T(8,128)(2,1)} %param.19, bf16[8,8,8,128]{3,2,1,0:T(8,128)(2,1)S(1)} %bitcast.78), kind=kOutput, calls=%fused_computation.30 | convolution fusion | flops 268435456 | bytes 4849664 | tf_op jit(solution)/shard_map/dot_general | solution.py:71
  79.0 0.1 eq.74
  79.1 0.2 convert_reduce_fusion
  79.3 0.1 reduce_sum.60
  79.4 0.1 fusion.43
  79.5 22.0 %reduce-scatter.2.cloned.1.call-done = f32[16,2048]{1,0:T(8,128)} async-done(((f32[64,2048]{1,0:T(8,128)}), f32[16,2048]{1,0:T(8,128)}) %reduce-scatter.2.cloned.1.call-update) | async-done | bytes 131088 | tf_op jit(solution)/shard_map/reduce_scatter | solution.py:70
  101.5 1.0 multiply_reduce_fusion
  102.6 2.4 %convolution_convert_fusion = bf16[256,2048]{1,0:T(8,128)(2,1)} fusion(pred[256,16]{0,1:T(8,128)(4,1)S(1)} %fusion.43, f32[2048]{0:T(1024)S(1)} %convert_element_type.37, f32[16]{0:T(128)S(1)} %add_rsqrt_fusion, f32[16,2048]{1,0:T(8,128)} %reduce-scatter.2.cloned.1.call-done, bf16[16,2048]{1,0:T(8,128)(2,1)S(1)} %copy-done.3), kind=kOutput, calls=%fused_computation.17 | convolution fusion | flops 17465344 | bytes 1257536 | tf_op jit(solution)/shard_map/dot_general | solution.py:93
  105.0 2.5 %reshape.170 = bf16[128,2,2048]{2,1,0:T(2,128)(2,1)} reshape(bf16[256,2048]{1,0:T(8,128)(2,1)} %convolution_convert_fusion) | data formatting | bytes 2097152 | tf_op jit(solution)/shard_map/reshape | solution.py:94
  107.6 30.3 %all_to_all.10 = bf16[128,2,2048]{2,1,0:T(2,128)(2,1)} all-to-all(bf16[128,2,2048]{2,1,0:T(2,128)(2,1)} %reshape.170), channel_id=1, replica_groups=mesh['req'=32,'kvh'=4] {'req','kvh'}, dimensions={0} | all-to-all | bytes 2097152 | tf_op jit(solution)/shard_map/all_to_all | solution.py:95
  137.8 2.3 %reshape.171 = bf16[256,2048]{1,0:T(8,128)(2,1)} reshape(bf16[128,2,2048]{2,1,0:T(2,128)(2,1)} %all_to_all.10) | data formatting | bytes 2097152 | tf_op jit(solution)/shard_map/reshape | solution.py:97
  140.1 4.1 %fusion.13 = f32[256,768]{1,0:T(8,128)} fusion(bf16[256,2048]{1,0:T(8,128)(2,1)} %reshape.171, bf16[1,2048,768]{2,1,0:T(8,128)(2,1)} %param.23), kind=kOutput, calls=%fused_computation.15 | convolution fusion | flops 805306368 | bytes 4980736 | tf_op jit(solution)/shard_map/dot_general | solution.py:98
  144.2 5.6 %fusion.15 = bf16[256,2048]{1,0:T(8,128)(2,1)} fusion(bf16[1,768,2048]{2,1,0:T(8,128)(2,1)S(1)} %copy-done, bf16[256,2048]{1,0:T(8,128)(2,1)} %reshape.171, bf16[1,2048,768]{2,1,0:T(8,128)(2,1)} %param.24, f32[256,768]{1,0:T(8,128)} %fusion.13), kind=kOutput, calls=%fused_computation.18 | convolution fusion | flops 1612120064 | bytes 9175040 | tf_op jit(solution)/shard_map/dot_general | solution.py:101
  149.8 2.6 %reshape.172 = bf16[128,2,2048]{2,1,0:T(2,128)(2,1)} reshape(bf16[256,2048]{1,0:T(8,128)(2,1)} %fusion.15) | data formatting | bytes 2097152 | tf_op jit(solution)/shard_map/reshape | solution.py:103
  152.3 4.7 %all-to-all-start.1 = ((bf16[128,2,2048]{2,1,0:T(2,128)(2,1)}), bf16[128,2,2048]{2,1,0:T(2,128)(2,1)}, u32[]{:S(2)}, u32[]{:S(2)}) async-start(bf16[128,2,2048]{2,1,0:T(2,128)(2,1)} %reshape.172), calls=%async_computation.2 | async-start | bytes 2097152 | tf_op jit(solution)/shard_map/all_to_all | solution.py:102
  157.1 0.1 copy.23
  157.2 19.3 %all-to-all-done.1 = bf16[128,2,2048]{2,1,0:T(2,128)(2,1)} async-done(((bf16[128,2,2048]{2,1,0:T(2,128)(2,1)}), bf16[128,2,2048]{2,1,0:T(2,128)(2,1)}, u32[]{:S(2)}, u32[]{:S(2)}) %all-to-all-start.1) | async-done | bytes 1048608 | tf_op jit(solution)/shard_map/all_to_all | solution.py:102
  176.5 2.3 %reshape.175 = bf16[256,2048,1]{1,0,2:T(8,128)(2,1)} reshape(bf16[128,2,2048]{2,1,0:T(2,128)(2,1)} %all-to-all-done.1) | data formatting | bytes 2097152 | tf_op jit(solution)/shard_map/reshape | solution.py:109
  178.8 1.7 fusion.26
  180.5 0.6 add_convert_fusion
  (29 shorter events, 0.2 us)
Async XLA Ops:
  6.5 137.7 %copy-start = (bf16[1,768,2048]{2,1,0:T(8,128)(2,1)S(1)}, bf16[1,768,2048]{2,1,0:T(8,128)(2,1)}, u32[]{:S(2)}) copy-start(bf16[1,768,2048]{2,1,0:T(8,128)(2,1)} %param.25) | copy-start | bytes 9437188
  6.5 7.0 %copy-start.8 = (s32[64]{0:T(128)S(1)}, s32[64]{0:T(128)}, u32[]{:S(2)}) copy-start(s32[64]{0:T(128)} %param.16) | copy-start | bytes 772
  6.5 95.0 %reduce-scatter.2.cloned.1.call-start = ((), (), s32[]{:S(2)}) async-start(), calls=%async_computation.3 | async-start | bytes 655360 | tf_op jit(solution)/shard_map/reduce_scatter | solution.py:70
  11.6 6.4 %copy-start.4 = (bf16[64,1,8,128]{3,2,1,0:T(8,128)(2,1)S(1)}, bf16[64,1,8,128]{3,2,1,0:T(8,128)(2,1)}, u32[]{:S(2)}) copy-start(bf16[64,1,8,128]{3,2,1,0:T(8,128)(2,1)} %param.13) | copy-start | bytes 393220
  17.9 18.7 %copy-start.1 = (pred[64,20480]{1,0:T(8,128)(4,1)}, pred[64,20480]{1,0:T(8,128)(4,1)S(1)}, u32[]{:S(2)}) copy-start(pred[64,20480]{1,0:T(8,128)(4,1)S(1)} %fusion.8) | copy-start | bytes 3932164
  75.0 3.9 %copy-start.6 = (s32[16,8]{0,1:T(8,128)S(1)}, s32[16,8]{0,1:T(8,128)}, u32[]{:S(2)}) copy-start(s32[16,8]{0,1:T(8,128)} %param.22) | copy-start | bytes 1540
  75.0 4.4 %copy-start.7 = (bf16[2048]{0:T(1024)(128)(2,1)S(1)}, bf16[2048]{0:T(1024)(128)(2,1)}, u32[]{:S(2)}) copy-start(bf16[2048]{0:T(1024)(128)(2,1)} %param.20) | copy-start | bytes 12292
  75.1 26.5 %copy-start.3 = (bf16[16,2048]{1,0:T(8,128)(2,1)S(1)}, bf16[16,2048]{1,0:T(8,128)(2,1)}, u32[]{:S(2)}) copy-start(bf16[16,2048]{1,0:T(8,128)(2,1)} %param.18) | copy-start | bytes 196612
  144.2 12.8 %copy-start.5 = (f32[16,8]{0,1:T(8,128)S(1)}, f32[16,8]{0,1:T(8,128)}, u32[]{:S(2)}) copy-start(f32[16,8]{0,1:T(8,128)} %param.21) | copy-start | bytes 1540
  149.8 30.7 %copy-start.2 = (f32[16,2048]{1,0:T(8,128)S(1)}, f32[16,2048]{1,0:T(8,128)}, u32[]{:S(2)}) copy-start(f32[16,2048]{1,0:T(8,128)} %reduce-scatter.2.cloned.1.call-done) | copy-start | bytes 393220
  152.3 24.1 %all-to-all-start.1 = ((bf16[128,2,2048]{2,1,0:T(2,128)(2,1)}), bf16[128,2,2048]{2,1,0:T(2,128)(2,1)}, u32[]{:S(2)}, u32[]{:S(2)}) async-start(bf16[128,2,2048]{2,1,0:T(2,128)(2,1)} %reshape.172), calls=%async_computation.2 | async-start | bytes 2097152 | tf_op jit(solution)/shard_map/all_to_all | solution.py:102
Sparse Core Ops, SparseCore 0:
  79.1 22.4 reduce-scatter.1
where the time goes:
time: 189 us; the launch traced here: 188 us
  matrix products  55 us (29%)
  waiting for transfers between devices  41.3 us (22%)
  blocking collectives  30.3 us (16%)
  other arithmetic  28.6 us (15%)
  local copies, waits for them, and re-layouts  14.5 us (8%)
  between operations  13.6 us (7%)
  starting transfers between devices  4.69 us (2%)
    all_to_all x1, blocking collectives, local(): lax.all_to_all(outgoing, ('req', 'kvh'), split_axis=0, concat_axis=0, til...  30.3 us
    reduce_scatter x1, waiting for transfers between devices, local(): lax.psum_scatter(jnp.dot(attended, w_out, preferred_element_type=jnp.floa...  22 us
    reduce_sum x1, other arithmetic, local(): denominator = jnp.sum(weights, axis=-1, keepdims=True)  19.6 us
    all_to_all x1, waiting for transfers between devices, local(): lax.all_to_all(produced.reshape(sources, width_slots, arrived_width), ('r...  19.3 us
    dot_general x1, matrix products, local(): jnp.einsum('qd,kd->qk', query_rows, key_rows, preferred_element_type=jnp....  18.7 us
    dot_general x1, matrix products, local(): jnp.dot(rounded, value_rows, preferred_element_type=jnp.float32)  18.6 us
    dot_general x1, matrix products, local(): jnp.dot(hidden, w_down[0], preferred_element_type=jnp.float32)  5.57 us
    all_to_all x1, starting transfers between devices, local(): lax.all_to_all(produced.reshape(sources, width_slots, arrived_width), ('r...  4.68 us
  transfers between devices with their start and end apart: 2, of which 2 were waited for; matrix products, arithmetic and copies ran while one was open for 0% of the time, Pallas kernels for 0%

commit v1 on v0

v1 whole, which is shorter than its diff:
```python
import functools

import jax
import jax.numpy as jnp
from jax import lax
from jax.experimental import pallas as pl
from jax.experimental.pallas import tpu as pltpu
from jax.sharding import PartitionSpec as P

AXES = ("req", "kvh")
BLOCK = 32
COLS = 4
FOLD = 4


def dot32(a, b):
    return jnp.dot(a, b, preferred_element_type=jnp.float32)


def stay(x):
    return pltpu.with_memory_space_constraint(x, pltpu.HBM)


def iota(shape, axis):
    return lax.broadcasted_iota(jnp.int32, shape, axis)


def attend_kernel(
    len_hbm, table_hbm, q_hbm, k_hbm, v_hbm, w_hbm, out_hbm,
    len_ref, table_ref, q_ref, k_buf, v_buf, w_buf, owner, left, m_ref, l_ref, o_ref, att_ref, out_buf,
    in_sem, k_sem, v_sem, out_sem,
):
    pages, slots, dim = k_buf.shape
    requests, groups, _ = q_ref.shape
    blocks = pages // BLOCK
    table_copies = (
        pltpu.make_async_copy(len_hbm, len_ref, in_sem.at[0]),
        pltpu.make_async_copy(table_hbm, table_ref, in_sem.at[1]),
    )
    q_copy = pltpu.make_async_copy(q_hbm, q_ref, in_sem.at[2])
    w_copy = pltpu.make_async_copy(w_hbm, w_buf, in_sem.at[3])
    for copy in table_copies:
        copy.start()
    q_copy.start()

    def copies(b):
        span = pl.ds(b * BLOCK, BLOCK)
        return (
            pltpu.make_async_copy(k_hbm.at[span], k_buf.at[span], k_sem.at[b]),
            pltpu.make_async_copy(v_hbm.at[span], v_buf.at[span], v_sem.at[b]),
        )

    for b in range(blocks):
        for copy in copies(b):
            copy.start()
    w_copy.start()
    m_ref[...] = jnp.full(m_ref.shape, -jnp.inf, jnp.float32)
    l_ref[...] = jnp.zeros(l_ref.shape, jnp.float32)
    o_ref[...] = jnp.zeros(o_ref.shape, jnp.float32)
    for copy in table_copies:
        copy.wait()

    @pl.loop(0, pages, unroll=8)
    def _(p):
        owner[p] = requests
        left[p] = 0

    @pl.loop(0, requests)
    def _(r):
        length = len_ref[r]

        @pl.loop(0, (length + slots - 1) >> (slots.bit_length() - 1))
        def _(j):
            p = table_ref[j, r]
            owner[p] = r
            left[p] = length - j * slots

    q_copy.wait()
    lane = iota((groups, slots), 1)

    @pl.loop(0, blocks)
    def _(b):
        for copy in copies(b):
            copy.wait()
        ids = [b * BLOCK + i for i in range(BLOCK)]
        own = [owner[p] for p in ids]
        scores, peaks = [], []
        for p, r in zip(ids, own):
            q = q_ref[jnp.minimum(r, requests - 1)]
            s = lax.dot_general(
                q, k_buf[p], (((1,), (1,)), ((), ())), preferred_element_type=jnp.float32
            ) * dim ** (-0.5)
            s = jnp.where(lane < left[p], s, -jnp.inf)
            scores.append(s)
            peaks.append(jnp.max(s, axis=-1, keepdims=True))
        shrink, weights = [], []
        for s, peak, r in zip(scores, peaks, own):
            old = m_ref[r]
            new = jnp.maximum(old, peak)
            m_ref[r] = new
            shrink.append(jnp.exp(old - new))
            weights.append(jnp.exp(s - new))
        for a, w, r, p in zip(shrink, weights, own, ids):
            mixed = dot32(w.astype(jnp.bfloat16), v_buf[p])
            l_ref[r] = a * l_ref[r] + w
            o_ref[r] = a * o_ref[r] + mixed

    for g in range(groups):
        total = jnp.sum(l_ref[:requests, g, :], axis=-1, keepdims=True)
        att_ref[:, g * dim:(g + 1) * dim] = (o_ref[:requests, g, :] / total).astype(jnp.bfloat16)
    w_copy.wait()
    att = att_ref[...]
    cols = out_buf.shape[1] // COLS
    writes = []
    for c in range(COLS):
        span = slice(c * cols, (c + 1) * cols)
        out_buf[:, span] = dot32(att, w_buf[:, span]).astype(out_buf.dtype)
        write = pltpu.make_async_copy(out_buf.at[:, span], out_hbm.at[:, span], out_sem.at[c])
        write.start()
        writes.append(write)
    for write in writes:
        write.wait()


def attend(lengths, page_table, queries, key_cache, value_cache, w_out):
    pages, slots, dim = key_cache.shape
    requests, groups, _ = queries.shape
    blocks = pages // BLOCK
    hbm = pl.BlockSpec(memory_space=pltpu.HBM)
    rows = (requests + 1, groups, dim)
    return pl.pallas_call(
        attend_kernel,
        out_shape=pltpu.HBM((requests, w_out.shape[1]), jnp.bfloat16),
        in_specs=[hbm] * 6,
        out_specs=hbm,
        scratch_shapes=[
            pltpu.SMEM(lengths.shape, jnp.int32),
            pltpu.SMEM(page_table.shape, jnp.int32),
            pltpu.VMEM(queries.shape, queries.dtype),
            pltpu.VMEM(key_cache.shape, key_cache.dtype),
            pltpu.VMEM(value_cache.shape, value_cache.dtype),
            pltpu.VMEM(w_out.shape, w_out.dtype),
            pltpu.SMEM((pages,), jnp.int32),
            pltpu.SMEM((pages,), jnp.int32),
            pltpu.VMEM(rows, jnp.float32),
            pltpu.VMEM(rows, jnp.float32),
            pltpu.VMEM(rows, jnp.float32),
            pltpu.VMEM((requests, groups * dim), jnp.bfloat16),
            pltpu.VMEM((requests, w_out.shape[1]), jnp.bfloat16),
            pltpu.SemaphoreType.DMA((4,)),
            pltpu.SemaphoreType.DMA((blocks,)),
            pltpu.SemaphoreType.DMA((blocks,)),
            pltpu.SemaphoreType.DMA((COLS,)),
        ],
        compiler_params=pltpu.CompilerParams(vmem_limit_bytes=24 << 20),
        name="attend",
    )(*map(stay, (lengths, page_table, queries, key_cache, value_cache, w_out)))


def plan_kernel(routes_t_ref, routes_ref, logits_ref, res_ref, send_ref, high_ref, low_ref, stay_ref):
    picks, tokens = routes_t_ref.shape
    rows, lanes = send_ref.shape
    stay_ref[...] = res_ref[...]
    src, dst = iota((lanes, lanes), 0), iota((lanes, lanes), 1)
    alike = (src & -tokens) == (dst & -tokens)
    before = ((src < dst) & alike).astype(jnp.float32).astype(jnp.bfloat16)
    after = ((src > dst) & alike).astype(jnp.float32).astype(jnp.bfloat16)

    spread = iota((tokens, lanes), 0) == (iota((tokens, lanes), 1) & (tokens - 1))
    named = dot32(
        routes_t_ref[...].astype(jnp.float32).astype(jnp.bfloat16),
        spread.astype(jnp.float32).astype(jnp.bfloat16),
    ).astype(jnp.int32)
    step = 256
    for start in range(0, rows, step):
        row = iota((step, lanes), 0) + start
        col = iota((step, lanes), 1)
        target = row >> 3
        has = named[0:1, :] == target
        for k in range(1, picks):
            has = has | (named[k:k + 1, :] == target)
        count = dot32(has.astype(jnp.float32).astype(jnp.bfloat16), before)
        fits = (count == (row & 1).astype(jnp.float32)) & (((row >> 1) & (FOLD - 1)) == col // tokens)
        send_ref[start:start + step, :] = (has & fits).astype(jnp.float32).astype(jnp.bfloat16)

    logits = logits_ref[...]
    raised = jnp.exp(logits - jnp.max(logits, axis=-1, keepdims=True))
    gates = raised / jnp.sum(raised, axis=-1, keepdims=True)
    gates = jnp.concatenate([gates] * FOLD, axis=0)
    routes = jnp.concatenate([routes_ref[...]] * FOLD, axis=0)
    for start in range(0, rows, step):
        col = iota((lanes, step), 1) + start
        row = iota((lanes, step), 0)
        target = col >> 3
        mix = jnp.zeros((lanes, step), jnp.float32)
        has = jnp.zeros((lanes, step), jnp.float32)
        for k in range(picks):
            same = routes[:, k:k + 1] == target
            mix = jnp.where(same, gates[:, k:k + 1], mix)
            has = jnp.where(same, 1.0, has)
        count = dot32(after, has.astype(jnp.bfloat16))
        fits = (count == (col & 1).astype(jnp.float32)) & (((col >> 1) & (FOLD - 1)) == row // tokens)
        mix = jnp.where(fits, mix, 0.0)
        high = mix.astype(jnp.bfloat16)
        high_ref[:, start:start + step] = high
        low_ref[:, start:start + step] = (mix - high.astype(jnp.float32)).astype(jnp.bfloat16)


def plan(routes, route_logits, residual, experts):
    tokens = routes.shape[0]
    rows, lanes = experts * 2 * FOLD, FOLD * tokens
    vmem = pl.BlockSpec(memory_space=pltpu.VMEM)
    return pl.pallas_call(
        plan_kernel,
        out_shape=(
            jax.ShapeDtypeStruct((rows, lanes), jnp.bfloat16),
            jax.ShapeDtypeStruct((lanes, rows), jnp.bfloat16),
            jax.ShapeDtypeStruct((lanes, rows), jnp.bfloat16),
            jax.ShapeDtypeStruct(residual.shape, residual.dtype),
        ),
        in_specs=[vmem] * 4,
        out_specs=(vmem,) * 4,
        compiler_params=pltpu.CompilerParams(vmem_limit_bytes=8 << 20),
        name="plan",
    )(routes.T, routes, route_logits, residual)


def dispatch_kernel(part_ref, res_ref, gain_ref, send_ref, stream_ref, out_ref):
    width = res_ref.shape[1]
    part = width // FOLD
    total = part_ref[0].astype(jnp.float32)
    for i in range(1, part_ref.shape[0]):
        total = total + part_ref[i].astype(jnp.float32)
    stream = res_ref[...].astype(jnp.float32) + total
    stream_ref[...] = stream
    inverse = lax.rsqrt(jnp.mean(stream * stream, axis=-1, keepdims=True) + 1e-06)
    normed = (stream * inverse * gain_ref[...].astype(jnp.float32)).astype(jnp.bfloat16)
    rows = jnp.concatenate([normed[:, f * part:(f + 1) * part] for f in range(FOLD)], axis=0)
    out_ref[...] = dot32(send_ref[...], rows).astype(out_ref.dtype)


def dispatch(parts, residual, gain, send):
    tokens, width = residual.shape
    vmem = pl.BlockSpec(memory_space=pltpu.VMEM)
    return pl.pallas_call(
        dispatch_kernel,
        out_shape=(
            jax.ShapeDtypeStruct((tokens, width), jnp.float32),
            jax.ShapeDtypeStruct((send.shape[0], width // FOLD), jnp.bfloat16),
        ),
        in_specs=[vmem] * 4,
        out_specs=(vmem, vmem),
        compiler_params=pltpu.CompilerParams(vmem_limit_bytes=8 << 20),
        name="dispatch",
    )(parts, residual, gain, send)


def expert_kernel(x_ref, gate_ref, up_hbm, down_hbm, out_ref, x_buf, up_ref, down_ref, sem):
    rows, part = x_ref.shape
    up_copy = pltpu.make_async_copy(up_hbm, up_ref, sem.at[0])
    down_copy = pltpu.make_async_copy(down_hbm, down_ref, sem.at[1])
    up_copy.start()
    down_copy.start()
    group = 128
    inner = group // FOLD
    j, i = iota((group, group), 0), iota((group, group), 1)

    def source(row):
        return ((row & (inner - 1)) >> 1) * (2 * FOLD) + (row // inner) * 2 + (row & 1)

    unfold = (i == source(j)).astype(jnp.float32).astype(jnp.bfloat16)
    refold = (j == source(i)).astype(jnp.float32).astype(jnp.bfloat16)
    for n in range(rows // group):
        piece = dot32(unfold, x_ref[n * group:(n + 1) * group, :]).astype(jnp.bfloat16)
        for f in range(FOLD):
            x_buf[n * inner:(n + 1) * inner, f * part:(f + 1) * part] = piece[f * inner:(f + 1) * inner]
    x = x_buf[...]
    gate = dot32(x, gate_ref[...])
    up_copy.wait()
    up = dot32(x, up_ref[...])
    hidden = (gate / (1.0 + jnp.exp(-gate)) * up).astype(jnp.bfloat16)
    down_copy.wait()
    made = dot32(hidden, down_ref[...]).astype(jnp.bfloat16)
    for n in range(rows // group):
        piece = jnp.concatenate(
            [made[n * inner:(n + 1) * inner, f * part:(f + 1) * part] for f in range(FOLD)], axis=0
        )
        out_ref[n * group:(n + 1) * group, :] = dot32(refold, piece).astype(out_ref.dtype)


def expert(arrived, w_gate, w_up, w_down):
    vmem = pl.BlockSpec(memory_space=pltpu.VMEM)
    hbm = pl.BlockSpec(memory_space=pltpu.HBM)
    rows, part = arrived.shape
    return pl.pallas_call(
        expert_kernel,
        out_shape=jax.ShapeDtypeStruct(arrived.shape, jnp.bfloat16),
        in_specs=[vmem, vmem, hbm, hbm],
        out_specs=vmem,
        scratch_shapes=[
            pltpu.VMEM((rows // FOLD, part * FOLD), jnp.bfloat16),
            pltpu.VMEM(w_up.shape, w_up.dtype),
            pltpu.VMEM(w_down.shape, w_down.dtype),
            pltpu.SemaphoreType.DMA((2,)),
        ],
        compiler_params=pltpu.CompilerParams(vmem_limit_bytes=32 << 20),
        name="expert",
    )(arrived, w_gate, stay(w_up), stay(w_down))


def combine_kernel(back_ref, stream_ref, high_ref, low_ref, out_ref):
    tokens = stream_ref.shape[0]
    part = back_ref.shape[1]
    back = back_ref[...]
    total = dot32(high_ref[...], back) + dot32(low_ref[...], back)
    for f in range(FOLD):
        span = slice(f * part, (f + 1) * part)
        out_ref[:, span] = (stream_ref[:, span] + total[f * tokens:(f + 1) * tokens]).astype(out_ref.dtype)


def combine(back, stream, high, low):
    vmem = pl.BlockSpec(memory_space=pltpu.VMEM)
    return pl.pallas_call(
        combine_kernel,
        out_shape=jax.ShapeDtypeStruct(stream.shape, jnp.bfloat16),
        in_specs=[vmem] * 4,
        out_specs=vmem,
        compiler_params=pltpu.CompilerParams(vmem_limit_bytes=8 << 20),
        name="combine",
    )(back, stream, high, low)


def local(
    queries,
    key_cache,
    value_cache,
    lengths,
    page_table,
    residual_in,
    w_out,
    norm_gain,
    route_logits,
    routes,
    w_gate,
    w_up,
    w_down,
):
    heads = lax.axis_size("kvh")
    experts = lax.axis_size("req") * heads
    partial = attend(lengths, page_table.T, queries[:, 0], key_cache[:, 0], value_cache[:, 0], w_out)
    tokens, width = residual_in.shape
    parts = lax.all_to_all(
        partial.reshape(heads, tokens, width), "kvh", split_axis=0, concat_axis=0, tiled=True
    )
    send, high, low, residual = plan(routes, route_logits, residual_in, experts)
    stream, outgoing = dispatch(parts, residual, norm_gain[None, :], send)
    layout = (experts, 2 * FOLD, width // FOLD)
    exchange = functools.partial(lax.all_to_all, axis_name=AXES, split_axis=0, concat_axis=0, tiled=True)
    arrived = exchange(outgoing.reshape(layout)).reshape(outgoing.shape)
    produced = expert(arrived, w_gate[0], w_up[0], w_down[0])
    back = exchange(produced.reshape(layout)).reshape(outgoing.shape)
    return combine(back, stream, high, low)


def solution(mesh):
    in_specs = (
        P("req", "kvh", None, None),
        P("req", "kvh", None, None),
        P("req", "kvh", None, None),
        P("req"),
        P("req", None),
        P(AXES, None),
        P("kvh", None),
        P(),
        P(AXES, None),
        P(AXES, None),
        P(AXES, None, None),
        P(AXES, None, None),
        P(AXES, None, None),
    )
    return jax.shard_map(
        local, mesh=mesh, in_specs=in_specs, out_specs=P(AXES, None), check_vma=False
    )
```

time: 189 us -> 84.3 us (0.45)
  matrix products: 55 us -> 0 us
  waiting for transfers between devices: 41.3 us -> 0.01 us
  other arithmetic: 28.6 us -> 0 us
  blocking collectives: 30.3 us -> 53.9 us
  Pallas kernels: 0 us -> 18 us
  between operations: 13.6 us -> 0.08 us
  local copies, waits for them, and re-layouts: 14.5 us -> 6.76 us
    dot_general x7 -> x0, matrix products: 55 us -> none  [the longest x1 18.7 us: local(): jnp.einsum('qd,kd->qk', query_rows, key_rows, preferred_element_type=jnp....]
    all_to_all x1 -> x2, blocking collectives: 30.3 us -> 53.9 us  [the longest x1 31.1 us: local(): arrived = exchange(outgoing.reshape(layout)).reshape(outgoing.shape)]
    reduce_scatter x1 -> x0, waiting for transfers between devices: 22 us -> none  [local(): lax.psum_scatter(jnp.dot(attended, w_out, preferred_element_type=jnp.floa...]
    reduce_sum x5 -> x0, other arithmetic: 21.9 us -> none  [the longest x1 19.6 us: local(): denominator = jnp.sum(weights, axis=-1, keepdims=True)]
    all_to_all x1, waiting for transfers between devices: 19.3 us -> 0.01 us  [local(): lax.all_to_all(partial.reshape(heads, tokens, width), 'kvh', split_axis=0...]
    pallas_call x0 -> x5, Pallas kernels: none -> 18 us  [the longest x1 9.58 us: attend(): pl.pallas_call(attend_kernel, out_shape=pltpu.HBM((requests, w_out.shape[...]
    reshape x4 -> x0, local copies, waits for them, and re-layouts: 9.65 us -> none  [the longest x1 2.58 us: local(): produced.reshape(sources, width_slots, arrived_width)]
    unnamed x20 -> x28, local copies, waits for them, and re-layouts: 1.08 us -> 6.75 us
  transfers between devices with their start and end apart: 2 -> 1, of which waited for: 2 -> 0; matrix products, arithmetic and copies ran while one was open for 0% -> 1% of each run, Pallas kernels for 0% -> 1%
where the time goes in v1:
time: 84.3 us; the launch traced here: 83.9 us
  blocking collectives  53.9 us (64%)
  Pallas kernels  18 us (21%)
  local copies, waits for them, and re-layouts  6.76 us (8%)
  starting transfers between devices  5.11 us (6%)
    all_to_all x1, blocking collectives, local(): arrived = exchange(outgoing.reshape(layout)).reshape(outgoing.shape)  31.1 us
    all_to_all x1, blocking collectives, local(): back = exchange(produced.reshape(layout)).reshape(outgoing.shape)  22.8 us
    pallas_call x1, Pallas kernels, attend(): pl.pallas_call(attend_kernel, out_shape=pltpu.HBM((requests, w_out.shape[...  9.58 us
    unnamed x28, local copies, waits for them, and re-layouts  6.75 us
    pallas_call x1, Pallas kernels, expert(): pl.pallas_call(expert_kernel, out_shape=jax.ShapeDtypeStruct(arrived.shap...  5.82 us
    all_to_all x1, starting transfers between devices, local(): lax.all_to_all(partial.reshape(heads, tokens, width), 'kvh', split_axis=0...  5.11 us
  transfers between devices with their start and end apart: 1, of which 0 were waited for; matrix products, arithmetic and copies ran while one was open for 1% of the time, Pallas kernels for 1%

profile of v1, /device:TPU:1, one launch (start us, length us, event | category | flops | bytes accessed | tf_op | source)
XLA Modules:
  0.0 83.9 jit_solution(17826869497002255778)
XLA Ops:
  0.0 0.0 copy-start.11
  0.0 0.0 copy-start.12
  0.0 0.0 copy-start.9
  0.0 9.6 %attend.1 = bf16[64,2048]{1,0:T(8,128)(2,1)} custom-call(s32[64]{0:T(128)} %len_hbm.1, s32[32,64]{1,0:T(8,128)} %bitcast.25, bf16[64,8,128]{2,1,0:T(8,128)(2,1)} %bitcast.24, bf16[160,128,128]{2,1,0:T(8,128)(2,1)} %bitcast.19, bf16[160,128,128]{2,1,0:T(8,128)(2,1)} %bitcast.20, bf16[1024,2048]{1,0:T(8,128)(2,1)} %w_hbm.1), custom_call_target="tpu_custom_call" | custom-call | tf_op jit(solution)/shard_map/attend/pallas_call | solution.py:131
  9.6 0.0 copy-start
  9.6 5.1 %all-to-all-start = ((bf16[4,16,2048]{2,1,0:T(8,128)(2,1)}), bf16[4,16,2048]{2,1,0:T(8,128)(2,1)S(1)}, u32[]{:S(2)}, u32[]{:S(2)}) async-start(bf16[4,16,2048]{2,1,0:T(8,128)(2,1)} %bitcast.23), calls=%async_computation | async-start | bytes 524288 | tf_op jit(solution)/shard_map/all_to_all | solution.py:352
  14.7 0.0 copy-done.11
  14.7 0.0 copy-done.12
  14.7 0.1 copy.15.logits_ref
  14.8 0.0 copy-done.9
  14.8 0.7 copy.14.routes_ref
  15.5 0.0 copy-start.7
  15.5 0.8 copy-done.7
  16.3 0.0 copy-start.8
  16.3 0.7 copy-done.8
  17.0 0.0 copy-start.10
  17.0 0.7 copy-done.10
  17.7 0.9 %plan.1 = (bf16[1024,64]{1,0:T(8,128)(2,1)S(1)}, bf16[64,1024]{1,0:T(8,128)(2,1)S(1)}, bf16[64,1024]{1,0:T(8,128)(2,1)S(1)}, bf16[16,2048]{1,0:T(8,128)(2,1)S(1)}) custom-call(s32[8,16]{1,0:T(8,128)S(1)} %bitcast.18, s32[16,8]{1,0:T(8,128)S(1)} %copy-done.8, f32[16,8]{1,0:T(8,128)S(1)} %copy.15.logits_ref, bf16[16,2048]{1,0:T(8,128)(2,1)S(1)} %copy-done.7), custom_call_target="tpu_custom_call" | custom-call | tf_op jit(solution)/shard_map/plan/pallas_call | solution.py:213
  18.6 0.0 copy-start.1
  18.6 0.7 copy-done.1
  19.3 0.7 copy-done.3
  20.0 0.6 copy-done.5
  20.6 0.0 all-to-all-done.part_ref
  20.6 0.9 %copy-done.2 = bf16[1024,64]{1,0:T(8,128)(2,1)S(1)} copy-done((bf16[1024,64]{1,0:T(8,128)(2,1)S(1)}, bf16[1024,64]{1,0:T(8,128)(2,1)}, u32[]{:S(2)}) %copy-start.2) | copy-done | bytes 131096
  21.6 0.8 copy-done.6
  22.4 0.5 dispatch.1
  23.0 31.1 %all_to_all.15 = bf16[128,8,512]{2,1,0:T(8,128)(2,1)S(1)} all-to-all(bf16[128,8,512]{2,1,0:T(8,128)(2,1)S(1)} %bitcast.17), channel_id=1, replica_groups=mesh['req'=32,'kvh'=4] {'req','kvh'}, dimensions={0} | all-to-all | bytes 2097152 | tf_op jit(solution)/shard_map/all_to_all | solution.py:359
  54.1 0.0 copy-done
  54.1 5.8 %expert.1 = bf16[1024,512]{1,0:T(8,128)(2,1)S(1)} custom-call(bf16[1024,512]{1,0:T(8,128)(2,1)S(1)} %bitcast.14, bf16[2048,768]{1,0:T(8,128)(2,1)S(1)} %bitcast.16, bf16[2048,768]{1,0:T(8,128)(2,1)} %bitcast.21, bf16[768,2048]{1,0:T(8,128)(2,1)} %bitcast.22), custom_call_target="tpu_custom_call" | custom-call | tf_op jit(solution)/shard_map/expert/pallas_call | solution.py:295
  59.9 22.8 %all_to_all.16 = bf16[128,8,512]{2,1,0:T(8,128)(2,1)S(1)} all-to-all(bf16[128,8,512]{2,1,0:T(8,128)(2,1)S(1)} %bitcast.15), channel_id=1, replica_groups=mesh['req'=32,'kvh'=4] {'req','kvh'}, dimensions={0} | all-to-all | bytes 2097152 | tf_op jit(solution)/shard_map/all_to_all | solution.py:361
  82.7 0.0 copy-done.4
  82.7 1.1 %combine.1 = bf16[16,2048]{1,0:T(8,128)(2,1)} custom-call(bf16[1024,512]{1,0:T(8,128)(2,1)S(1)} %bitcast.13, f32[16,2048]{1,0:T(8,128)S(1)} %get-tuple-element.14.stream_ref, bf16[64,1024]{1,0:T(8,128)(2,1)S(1)} %get-tuple-element.15.high_ref, bf16[64,1024]{1,0:T(8,128)(2,1)S(1)} %copy-done.4), custom_call_target="tpu_custom_call" | custom-call | tf_op jit(solution)/shard_map/combine/pallas_call | solution.py:323
  (6 shorter events, 0.0 us)
Async XLA Ops:
  0.0 14.7 %copy-start.11 = (bf16[2048]{0:T(1024)(128)(2,1)S(1)}, bf16[2048]{0:T(1024)(128)(2,1)}, u32[]{:S(2)}) copy-start(bf16[2048]{0:T(1024)(128)(2,1)} %param.20) | copy-start | bytes 12292
  0.0 14.7 %copy-start.12 = (f32[16,8]{0,1:T(8,128)S(1)}, f32[16,8]{0,1:T(8,128)}, u32[]{:S(2)}) copy-start(f32[16,8]{0,1:T(8,128)} %param.21) | copy-start | bytes 1540
  0.0 14.8 %copy-start.9 = (s32[16,8]{0,1:T(8,128)S(1)}, s32[16,8]{0,1:T(8,128)}, u32[]{:S(2)}) copy-start(s32[16,8]{0,1:T(8,128)} %param.22) | copy-start | bytes 1540
  9.6 44.5 %copy-start = (bf16[1,2048,768]{2,1,0:T(8,128)(2,1)S(1)}, bf16[1,2048,768]{2,1,0:T(8,128)(2,1)}, u32[]{:S(2)}) copy-start(bf16[1,2048,768]{2,1,0:T(8,128)(2,1)} %param.23) | copy-start | bytes 9437188
  9.6 11.0 %all-to-all-start = ((bf16[4,16,2048]{2,1,0:T(8,128)(2,1)}), bf16[4,16,2048]{2,1,0:T(8,128)(2,1)S(1)}, u32[]{:S(2)}, u32[]{:S(2)}) async-start(bf16[4,16,2048]{2,1,0:T(8,128)(2,1)} %bitcast.23), calls=%async_computation | async-start | bytes 524288 | tf_op jit(solution)/shard_map/all_to_all | solution.py:352
  15.5 0.8 %copy-start.7 = (bf16[16,2048]{1,0:T(8,128)(2,1)S(1)}, bf16[16,2048]{1,0:T(8,128)(2,1)}, u32[]{:S(2)}) copy-start(bf16[16,2048]{1,0:T(8,128)(2,1)} %res_ref.1) | copy-start | bytes 196612
  16.3 0.7 copy-start.8
  17.0 0.7 copy-start.10
  18.6 0.7 copy-start.1
  19.3 0.7 copy-start.3
  20.0 0.6 copy-start.5
  20.6 1.0 %copy-start.2 = (bf16[1024,64]{1,0:T(8,128)(2,1)S(1)}, bf16[1024,64]{1,0:T(8,128)(2,1)}, u32[]{:S(2)}) copy-start(bf16[1024,64]{1,0:T(8,128)(2,1)} %copy-done.1) | copy-start | bytes 393220
  21.6 0.8 %copy-start.6 = (bf16[16,2048]{1,0:T(8,128)(2,1)S(1)}, bf16[16,2048]{1,0:T(8,128)(2,1)}, u32[]{:S(2)}) copy-start(bf16[16,2048]{1,0:T(8,128)(2,1)} %copy-done.5) | copy-start | bytes 196612
  54.1 28.7 %copy-start.4 = (bf16[64,1024]{1,0:T(8,128)(2,1)S(1)}, bf16[64,1024]{1,0:T(8,128)(2,1)}, u32[]{:S(2)}) copy-start(bf16[64,1024]{1,0:T(8,128)(2,1)} %copy-done.3) | copy-start | bytes 393220

commit v2 on v1

v2 whole, which is shorter than its diff:
```python
import functools

import jax
import jax.numpy as jnp
from jax import lax
from jax.experimental import pallas as pl
from jax.experimental.pallas import tpu as pltpu
from jax.sharding import PartitionSpec as P

AXES = ("req", "kvh")
BLOCK = 80
COLS = 4
FOLD = 4


def dot32(a, b):
    return jnp.dot(a, b, preferred_element_type=jnp.float32)


def stay(x):
    return pltpu.with_memory_space_constraint(x, pltpu.HBM)


def dot_t(a, b):
    return lax.dot_general(a, b, (((1,), (1,)), ((), ())), preferred_element_type=jnp.float32)


def flags(mask):
    return mask.astype(jnp.float32).astype(jnp.bfloat16)


def iota(shape, axis):
    return lax.broadcasted_iota(jnp.int32, shape, axis)


def plan(routes, gates, send_ref, mix_ref):
    picks, tokens = routes.shape
    rows, lanes = send_ref.shape
    experts = rows // (2 * FOLD)
    spread = flags(iota((lanes, tokens), 1) == (iota((lanes, tokens), 0) & (tokens - 1)))
    high = gates.astype(jnp.bfloat16)
    low = (gates - high.astype(jnp.float32)).astype(jnp.bfloat16)
    named = dot_t(spread, routes.astype(jnp.float32).astype(jnp.bfloat16))
    highs, lows = dot_t(spread, high), dot_t(spread, low)
    expert = iota((lanes, experts), 1).astype(jnp.float32)
    has = jnp.zeros((lanes, experts), jnp.float32)
    mix_high, mix_low = has, has
    for k in range(picks):
        match = named[:, k:k + 1] == expert
        has = jnp.where(match, 1.0, has)
        mix_high = jnp.where(match, highs[:, k:k + 1], mix_high)
        mix_low = jnp.where(match, lows[:, k:k + 1], mix_low)
    dst, src = iota((lanes, lanes), 0), iota((lanes, lanes), 1)
    before = flags((src < dst) & ((src & -tokens) == (dst & -tokens)))
    count = dot32(before, has.astype(jnp.bfloat16))

    pieces = 4
    span, step = experts // pieces, rows // pieces
    row, col = iota((step, 2 * span), 0), iota((step, 2 * span), 1)
    place = flags(((row & 1) * span + (row >> 3)) == col)
    keep = ((iota((step, lanes), 0) >> 1) & (FOLD - 1)) == iota((step, lanes), 1) // tokens
    row, col = iota((2 * span, step), 0), iota((2 * span, step), 1)
    place_t = flags(((col & 1) * span + (col >> 3)) == row)
    keep_t = ((iota((2 * lanes, step), 1) >> 1) & (FOLD - 1)) == (iota((2 * lanes, step), 0) & (lanes - 1)) // tokens

    def by_slot(values, n):
        part = slice(n * span, (n + 1) * span)
        return jnp.concatenate(
            [jnp.where(count[:, part] == float(c), values[:, part], 0.0) for c in range(2)], axis=1
        ).astype(jnp.bfloat16)

    for n in range(pieces):
        out = slice(n * step, (n + 1) * step)
        sends = dot_t(place, by_slot(has, n))
        send_ref[out, :] = jnp.where(keep, sends, 0.0).astype(jnp.bfloat16)
        mixes = jnp.concatenate([by_slot(mix_high, n), by_slot(mix_low, n)], axis=0)
        mix_ref[:, out] = jnp.where(keep_t, dot32(mixes, place_t), 0.0).astype(jnp.bfloat16)


def attend_kernel(
    len_hbm, table_hbm, q_hbm, k_hbm, v_hbm, w_hbm, routes_hbm, logits_hbm, res_hbm, gain_hbm,
    out_ref, send_ref, mix_ref, res_ref, gain_ref,
    len_ref, table_ref, q_ref, k_buf, v_buf, w_buf, routes_ref, logits_ref,
    apart_ref, left_ref, s_ref, m_ref, o_ref, att_ref,
    in_sem, k_sem, v_sem, w_sem,
):
    pages, slots, dim = k_buf.shape
    requests, groups, _ = q_ref.shape
    columns = table_ref.shape[0]
    blocks = pages // BLOCK
    cols = out_ref.shape[1] // COLS

    def fetch(n, src, dst):
        return pltpu.make_async_copy(src, dst, in_sem.at[n])

    small = [
        fetch(0, len_hbm, len_ref), fetch(1, table_hbm, table_ref), fetch(2, q_hbm, q_ref),
        fetch(3, routes_hbm, routes_ref), fetch(4, logits_hbm, logits_ref),
        fetch(5, res_hbm, res_ref), fetch(6, gain_hbm, gain_ref),
    ]
    k_copies, v_copies = [], []
    for b in range(blocks):
        span = pl.ds(b * BLOCK, BLOCK)
        k_copies.append(pltpu.make_async_copy(k_hbm.at[span], k_buf.at[span], k_sem.at[b]))
        v_copies.append(pltpu.make_async_copy(v_hbm.at[span], v_buf.at[span], v_sem.at[b]))
    w_copies = []
    for c in range(COLS):
        span = slice(c * cols, (c + 1) * cols)
        w_copies.append(pltpu.make_async_copy(w_hbm.at[:, span], w_buf.at[:, span], w_sem.at[c]))
    for copy in small[:3] + k_copies + small[3:] + v_copies + w_copies:
        copy.start()

    small[0].wait()
    small[1].wait()
    lengths = len_ref[...]
    column = iota((columns, requests), 0)
    table = jnp.where(column < ((lengths + (slots - 1)) >> (slots.bit_length() - 1)), table_ref[...], -1)
    usable = lengths - column * slots
    half = columns // 2
    table = jnp.concatenate([table[:half], table[half:]], axis=1)
    usable = jnp.concatenate([usable[:half], usable[half:]], axis=1)
    page = iota((pages, 2 * requests), 0)
    left = jnp.zeros((pages, 2 * requests), jnp.int32)
    for c in range(half):
        left = jnp.where(table[c:c + 1, :] == page, usable[c:c + 1, :], left)
    left = left.astype(jnp.float32)
    owned = jnp.maximum(left[:, :requests], left[:, requests:]) > 0
    left_ref[...] = jnp.broadcast_to(jnp.max(left, axis=-1, keepdims=True), left_ref.shape)
    apart_ref[...] = jnp.where(owned, 0.0, -jnp.inf)
    owned = flags(owned)
    same = flags(iota((requests, requests), 0) == iota((requests, requests), 1))
    pick = dot_t(same, owned).astype(jnp.bfloat16)

    def pair_rows(p):
        return pl.ds(p * groups, 2 * groups)

    def apart_rows(x):
        top = iota(x.shape, 0) < groups
        return jnp.concatenate([jnp.where(top, x, 0.0), jnp.where(top, 0.0, x)], axis=1).astype(jnp.bfloat16)

    def group_rows(g, count):
        return pl.ds(g, count, stride=groups)

    small[2].wait()
    o_ref[:requests * groups, :] = q_ref[...].reshape(requests * groups, dim).astype(jnp.float32)
    for g in range(groups):
        s_ref[group_rows(g, pages), :] = dot32(owned, o_ref[group_rows(g, requests), :].astype(jnp.bfloat16))

    lane = iota((2 * groups, slots), 1).astype(jnp.float32)
    for b in range(blocks):
        k_copies[b].wait()

        for p in range(b * BLOCK, (b + 1) * BLOCK, 2):
            keys = jnp.concatenate([k_buf[p], k_buf[p + 1]], axis=1)
            s = dot_t(apart_rows(s_ref[pair_rows(p), :]), keys) * dim ** (-0.5)
            limit = jnp.concatenate(
                [left_ref[pl.ds(p + i, groups, stride=0), :] for i in range(2)], axis=0
            )
            s = jnp.where(lane < limit, s, -jnp.inf)
            s_ref[pair_rows(p), :] = s
            m_ref[pair_rows(p), :] = jnp.broadcast_to(jnp.max(s, axis=-1, keepdims=True), s.shape)

    apart = apart_ref[...]
    for g in range(groups):
        peak = jnp.max(m_ref[group_rows(g, pages), :][:, :requests] + apart, axis=0, keepdims=True)
        peak = jnp.maximum(jnp.max(peak + apart, axis=-1, keepdims=True), -3e38)
        m_ref[group_rows(g, pages), :] = jnp.broadcast_to(peak, (pages, dim))

    for copy in small[3:]:
        copy.wait()
    logits = logits_ref[...]
    raised = jnp.exp(logits - jnp.max(logits, axis=0, keepdims=True))
    plan(
        routes_ref[...], raised / jnp.sum(raised, axis=0, keepdims=True), send_ref, mix_ref
    )

    for b in range(blocks):
        v_copies[b].wait()

        for p in range(b * BLOCK, (b + 1) * BLOCK, 2):
            w = jnp.exp(s_ref[pair_rows(p), :] - m_ref[pair_rows(p), :])
            m_ref[pair_rows(p), :] = jnp.broadcast_to(jnp.sum(w, axis=-1, keepdims=True), w.shape)
            values = jnp.concatenate([v_buf[p], v_buf[p + 1]], axis=0)
            o_ref[pair_rows(p), :] = dot32(apart_rows(w), values)

    def parts(values):
        high = values.astype(jnp.bfloat16).astype(jnp.float32)
        return high, values - high

    first = iota((pages, dim), 1) < dim // 2
    for g in range(groups):
        high, low = parts(o_ref[group_rows(g, pages), :])
        sums = jnp.where(first, *parts(m_ref[group_rows(g, pages), :]))
        total = dot32(pick, jnp.concatenate([high, low, sums], axis=1).astype(jnp.bfloat16))
        weight = total[:, 2 * dim:]
        weight = weight + pltpu.roll(weight, dim // 2, 1)
        att_ref[:, g * dim:(g + 1) * dim] = (
            (total[:, :dim] + total[:, dim:2 * dim]) / weight
        ).astype(jnp.bfloat16)

    att = att_ref[...]
    for c in range(COLS):
        span = slice(c * cols, (c + 1) * cols)
        w_copies[c].wait()
        out_ref[:, span] = dot32(att, w_buf[:, span]).astype(out_ref.dtype)


def attend(lengths, page_table, queries, key_cache, value_cache, w_out, routes, logits, residual, gain, experts):
    pages, slots, dim = key_cache.shape
    requests, groups, _ = queries.shape
    tokens = residual.shape[0]
    blocks = pages // BLOCK
    hbm = pl.BlockSpec(memory_space=pltpu.HBM)
    vmem = pl.BlockSpec(memory_space=pltpu.VMEM)
    rows, lanes = experts * 2 * FOLD, FOLD * tokens
    tile = pltpu.VMEM((pages * groups, dim), jnp.float32)
    args = (lengths, page_table, queries, key_cache, value_cache, w_out, routes, logits, residual, gain)
    return pl.pallas_call(
        attend_kernel,
        out_shape=(
            jax.ShapeDtypeStruct((requests, w_out.shape[1]), jnp.bfloat16),
            jax.ShapeDtypeStruct((rows, lanes), jnp.bfloat16),
            jax.ShapeDtypeStruct((2 * lanes, rows), jnp.bfloat16),
            jax.ShapeDtypeStruct(residual.shape, residual.dtype),
            jax.ShapeDtypeStruct(gain.shape, gain.dtype),
        ),
        in_specs=[hbm] * len(args),
        out_specs=(vmem,) * 5,
        scratch_shapes=[
            pltpu.VMEM(lengths.shape, jnp.int32),
            pltpu.VMEM(page_table.shape, jnp.int32),
            pltpu.VMEM(queries.shape, queries.dtype),
            pltpu.VMEM(key_cache.shape, key_cache.dtype),
            pltpu.VMEM(value_cache.shape, value_cache.dtype),
            pltpu.VMEM(w_out.shape, w_out.dtype),
            pltpu.VMEM(routes.shape, jnp.int32),
            pltpu.VMEM(logits.shape, jnp.float32),
            pltpu.VMEM((pages, requests), jnp.float32),
            pltpu.VMEM((pages, slots), jnp.float32),
            tile, tile, tile,
            pltpu.VMEM((requests, groups * dim), jnp.bfloat16),
            pltpu.SemaphoreType.DMA((7,)),
            pltpu.SemaphoreType.DMA((blocks,)),
            pltpu.SemaphoreType.DMA((blocks,)),
            pltpu.SemaphoreType.DMA((COLS,)),
        ],
        compiler_params=pltpu.CompilerParams(vmem_limit_bytes=24 << 20),
        name="attend",
    )(*map(stay, args))


def dispatch_kernel(part_ref, res_ref, gain_ref, send_ref, stream_ref, out_ref):
    width = res_ref.shape[1]
    part = width // FOLD
    total = part_ref[0].astype(jnp.float32)
    for i in range(1, part_ref.shape[0]):
        total = total + part_ref[i].astype(jnp.float32)
    stream = res_ref[...].astype(jnp.float32) + total
    stream_ref[...] = stream
    inverse = lax.rsqrt(jnp.mean(stream * stream, axis=-1, keepdims=True) + 1e-06)
    gain = gain_ref[...].astype(jnp.float32)
    gain = jnp.concatenate([gain[i:i + 1] for i in range(gain.shape[0])], axis=1)
    normed = (stream * inverse * gain).astype(jnp.bfloat16)
    rows = jnp.concatenate([normed[:, f * part:(f + 1) * part] for f in range(FOLD)], axis=0)
    out_ref[...] = dot32(send_ref[...], rows).astype(out_ref.dtype)


def dispatch(parts, residual, gain, send):
    tokens, width = residual.shape
    vmem = pl.BlockSpec(memory_space=pltpu.VMEM)
    return pl.pallas_call(
        dispatch_kernel,
        out_shape=(
            jax.ShapeDtypeStruct((tokens, width), jnp.float32),
            jax.ShapeDtypeStruct((send.shape[0], width // FOLD), jnp.bfloat16),
        ),
        in_specs=[vmem] * 4,
        out_specs=(vmem, vmem),
        compiler_params=pltpu.CompilerParams(vmem_limit_bytes=8 << 20),
        name="dispatch",
    )(parts, residual, gain, send)


def expert_kernel(x_ref, gate_ref, up_ref, down_ref, out_ref, x_buf):
    rows, part = x_ref.shape
    group = 128
    inner = group // FOLD
    j, i = iota((group, group), 0), iota((group, group), 1)

    def source(row):
        return ((row & (inner - 1)) >> 1) * (2 * FOLD) + (row // inner) * 2 + (row & 1)

    unfold = (i == source(j)).astype(jnp.float32).astype(jnp.bfloat16)
    refold = (j == source(i)).astype(jnp.float32).astype(jnp.bfloat16)
    for n in range(rows // group):
        piece = dot32(unfold, x_ref[n * group:(n + 1) * group, :]).astype(jnp.bfloat16)
        for f in range(FOLD):
            x_buf[n * inner:(n + 1) * inner, f * part:(f + 1) * part] = piece[f * inner:(f + 1) * inner]
    x = x_buf[...]
    gate = dot32(x, gate_ref[...])
    up = dot32(x, up_ref[...])
    hidden = (gate / (1.0 + jnp.exp(-gate)) * up).astype(jnp.bfloat16)
    made = dot32(hidden, down_ref[...]).astype(jnp.bfloat16)
    for n in range(rows // group):
        piece = jnp.concatenate(
            [made[n * inner:(n + 1) * inner, f * part:(f + 1) * part] for f in range(FOLD)], axis=0
        )
        out_ref[n * group:(n + 1) * group, :] = dot32(refold, piece).astype(out_ref.dtype)


def expert(arrived, w_gate, w_up, w_down):
    vmem = pl.BlockSpec(memory_space=pltpu.VMEM)
    hbm = pl.BlockSpec(memory_space=pltpu.HBM)
    rows, part = arrived.shape
    return pl.pallas_call(
        expert_kernel,
        out_shape=jax.ShapeDtypeStruct(arrived.shape, jnp.bfloat16),
        in_specs=[vmem] * 4,
        out_specs=vmem,
        scratch_shapes=[
            pltpu.VMEM((rows // FOLD, part * FOLD), jnp.bfloat16),
        ],
        compiler_params=pltpu.CompilerParams(vmem_limit_bytes=16 << 20),
        name="expert",
    )(arrived, w_gate, w_up, w_down)


def combine_kernel(back_ref, stream_ref, mix_ref, out_ref):
    tokens = stream_ref.shape[0]
    part = back_ref.shape[1]
    total = dot32(mix_ref[...], back_ref[...])
    total = total[:FOLD * tokens] + total[FOLD * tokens:]
    for f in range(FOLD):
        span = slice(f * part, (f + 1) * part)
        out_ref[:, span] = (stream_ref[:, span] + total[f * tokens:(f + 1) * tokens]).astype(out_ref.dtype)


def combine(back, stream, mix):
    vmem = pl.BlockSpec(memory_space=pltpu.VMEM)
    return pl.pallas_call(
        combine_kernel,
        out_shape=jax.ShapeDtypeStruct(stream.shape, jnp.bfloat16),
        in_specs=[vmem] * 3,
        out_specs=vmem,
        compiler_params=pltpu.CompilerParams(vmem_limit_bytes=8 << 20),
        name="combine",
    )(back, stream, mix)


def local(
    queries,
    key_cache,
    value_cache,
    lengths,
    page_table,
    residual_in,
    w_out,
    norm_gain,
    route_logits,
    routes,
    w_gate,
    w_up,
    w_down,
):
    heads = lax.axis_size("kvh")
    experts = lax.axis_size("req") * heads
    tokens, width = residual_in.shape
    partial, send, mix, residual, gain = attend(
        lengths[None, :], page_table.T, queries[:, 0], key_cache[:, 0], value_cache[:, 0], w_out,
        routes.T, route_logits.T, residual_in, norm_gain.reshape(-1, 128), experts,
    )
    parts = lax.all_to_all(
        partial.reshape(heads, tokens, width), "kvh", split_axis=0, concat_axis=0, tiled=True
    )
    stream, outgoing = dispatch(parts, residual, gain, send)
    layout = (experts, 2 * FOLD, width // FOLD)
    exchange = functools.partial(lax.all_to_all, axis_name=AXES, split_axis=0, concat_axis=0, tiled=True)
    arrived = exchange(outgoing.reshape(layout)).reshape(outgoing.shape)
    produced = expert(arrived, w_gate[0], w_up[0], w_down[0])
    back = exchange(produced.reshape(layout)).reshape(outgoing.shape)
    return combine(back, stream, mix)


def solution(mesh):
    in_specs = (
        P("req", "kvh", None, None),
        P("req", "kvh", None, None),
        P("req", "kvh", None, None),
        P("req"),
        P("req", None),
        P(AXES, None),
        P("kvh", None),
        P(),
        P(AXES, None),
        P(AXES, None),
        P(AXES, None, None),
        P(AXES, None, None),
        P(AXES, None, None),
    )
    return jax.shard_map(
        local, mesh=mesh, in_specs=in_specs, out_specs=P(AXES, None), check_vma=False
    )
```

time: 84.3 us -> 77.1 us (0.915)
  blocking collectives: 53.9 us -> 63 us
  local copies, waits for them, and re-layouts: 6.76 us -> 0.01 us
  starting transfers between devices: 5.11 us -> 0 us
  Pallas kernels: 18 us -> 13.9 us
    all_to_all x0 -> x1, blocking collectives: none -> 10.5 us  [local(): lax.all_to_all(partial.reshape(heads, tokens, width), 'kvh', split_axis=0...]
    unnamed x28 -> x6, local copies, waits for them, and re-layouts: 6.75 us -> 0.01 us
    all_to_all x1 -> x0, starting transfers between devices: 5.11 us -> none  [local(): lax.all_to_all(partial.reshape(heads, tokens, width), 'kvh', split_axis=0...]
    pallas_call x1, Pallas kernels: 5.82 us -> 3.25 us  [expert(): pl.pallas_call(expert_kernel, out_shape=jax.ShapeDtypeStruct(arrived.shap...]
    pallas_call x2 -> x1, Pallas kernels: 10.5 us -> 9.12 us  [attend(): pl.pallas_call(attend_kernel, out_shape=(jax.ShapeDtypeStruct((requests,...]
    all_to_all x1, blocking collectives: 31.1 us -> 29.7 us  [local(): arrived = exchange(outgoing.reshape(layout)).reshape(outgoing.shape)]
  transfers between devices with their start and end apart: 1 -> 0, of which waited for: 0 -> 0; matrix products, arithmetic and copies ran while one was open for 1% -> 0% of each run, Pallas kernels for 1% -> 0%
where the time goes in v2:
time: 77.1 us; the launch traced here: 76.9 us
  blocking collectives  63 us (82%)
  Pallas kernels  13.9 us (18%)
    all_to_all x1, blocking collectives, local(): arrived = exchange(outgoing.reshape(layout)).reshape(outgoing.shape)  29.7 us
    all_to_all x1, blocking collectives, local(): back = exchange(produced.reshape(layout)).reshape(outgoing.shape)  22.8 us
    all_to_all x1, blocking collectives, local(): lax.all_to_all(partial.reshape(heads, tokens, width), 'kvh', split_axis=0...  10.5 us
    pallas_call x1, Pallas kernels, attend(): pl.pallas_call(attend_kernel, out_shape=(jax.ShapeDtypeStruct((requests,...  9.12 us
    pallas_call x1, Pallas kernels, expert(): pl.pallas_call(expert_kernel, out_shape=jax.ShapeDtypeStruct(arrived.shap...  3.25 us

profile of v2, /device:TPU:1, one launch (start us, length us, event | category | flops | bytes accessed | tf_op | source)
XLA Modules:
  0.0 76.9 jit_solution(13615432639073717991)
XLA Ops:
  0.0 0.0 copy-start.1
  0.0 0.0 copy-start.2
  0.0 9.1 %attend.1 = (bf16[64,2048]{1,0:T(8,128)(2,1)S(1)}, bf16[1024,64]{1,0:T(8,128)(2,1)S(1)}, bf16[128,1024]{1,0:T(8,128)(2,1)S(1)}, bf16[16,2048]{1,0:T(8,128)(2,1)S(1)}, bf16[16,128]{1,0:T(8,128)(2,1)S(1)}) custom-call(s32[1,64]{1,0:T(1,128)} %bitcast.31, s32[32,64]{1,0:T(8,128)} %bitcast.27, bf16[64,8,128]{2,1,0:T(8,128)(2,1)} %bitcast.26, ...), custom_call_target="tpu_custom_call" | custom-call | tf_op jit(solution)/shard_map/attend/pallas_call | solution.py:218
  9.1 0.0 copy-start
  9.1 10.5 %all_to_all.15.part_ref = bf16[4,16,2048]{2,1,0:T(8,128)(2,1)S(1)} all-to-all(bf16[4,16,2048]{2,1,0:T(8,128)(2,1)S(1)} %bitcast.23), channel_id=1, replica_groups=mesh['req'=32,'kvh'=4] {'kvh'}, dimensions={0} | all-to-all | bytes 524288 | tf_op jit(solution)/shard_map/all_to_all | solution.py:372
  19.6 0.6 dispatch.1
  20.2 29.7 %all_to_all.16 = bf16[128,8,512]{2,1,0:T(8,128)(2,1)S(1)} all-to-all(bf16[128,8,512]{2,1,0:T(8,128)(2,1)S(1)} %bitcast.22), channel_id=1, replica_groups=mesh['req'=32,'kvh'=4] {'req','kvh'}, dimensions={0} | all-to-all | bytes 2097152 | tf_op jit(solution)/shard_map/all_to_all | solution.py:378
  49.9 0.0 copy-done.1
  49.9 0.0 copy-done.2
  49.9 0.0 copy-done
  49.9 3.3 %expert.1 = bf16[1024,512]{1,0:T(8,128)(2,1)S(1)} custom-call(bf16[1024,512]{1,0:T(8,128)(2,1)S(1)} %bitcast.17, bf16[2048,768]{1,0:T(8,128)(2,1)S(1)} %bitcast.19, bf16[2048,768]{1,0:T(8,128)(2,1)S(1)} %bitcast.20, bf16[768,2048]{1,0:T(8,128)(2,1)S(1)} %bitcast.21), custom_call_target="tpu_custom_call" | custom-call | tf_op jit(solution)/shard_map/expert/pallas_call | solution.py:315
  53.2 22.8 %all_to_all.17 = bf16[128,8,512]{2,1,0:T(8,128)(2,1)S(1)} all-to-all(bf16[128,8,512]{2,1,0:T(8,128)(2,1)S(1)} %bitcast.18), channel_id=1, replica_groups=mesh['req'=32,'kvh'=4] {'req','kvh'}, dimensions={0} | all-to-all | bytes 2097152 | tf_op jit(solution)/shard_map/all_to_all | solution.py:380
  76.0 0.9 %combine.1 = bf16[16,2048]{1,0:T(8,128)(2,1)} custom-call(bf16[1024,512]{1,0:T(8,128)(2,1)S(1)} %bitcast.16, f32[16,2048]{1,0:T(8,128)S(1)} %get-tuple-element.17.stream_ref, bf16[128,1024]{1,0:T(8,128)(2,1)S(1)} %get-tuple-element.18.mix_ref), custom_call_target="tpu_custom_call" | custom-call | tf_op jit(solution)/shard_map/combine/pallas_call | solution.py:340
Async XLA Ops:
  0.0 49.9 %copy-start.1 = (bf16[1,2048,768]{2,1,0:T(8,128)(2,1)S(1)}, bf16[1,2048,768]{2,1,0:T(8,128)(2,1)}, u32[]{:S(2)}) copy-start(bf16[1,2048,768]{2,1,0:T(8,128)(2,1)} %param.24) | copy-start | bytes 9437188
  0.0 49.9 %copy-start.2 = (bf16[1,768,2048]{2,1,0:T(8,128)(2,1)S(1)}, bf16[1,768,2048]{2,1,0:T(8,128)(2,1)}, u32[]{:S(2)}) copy-start(bf16[1,768,2048]{2,1,0:T(8,128)(2,1)} %param.25) | copy-start | bytes 9437188
  9.1 40.8 %copy-start = (bf16[1,2048,768]{2,1,0:T(8,128)(2,1)S(1)}, bf16[1,2048,768]{2,1,0:T(8,128)(2,1)}, u32[]{:S(2)}) copy-start(bf16[1,2048,768]{2,1,0:T(8,128)(2,1)} %param.23) | copy-start | bytes 9437188

commit v3 on v2

--- a/solution.py
+++ b/solution.py
@@ -37,21 +37,20 @@
     picks, tokens = routes.shape
     rows, lanes = send_ref.shape
     experts = rows // (2 * FOLD)
-    spread = flags(iota((lanes, tokens), 1) == (iota((lanes, tokens), 0) & (tokens - 1)))
+    same = flags(iota((tokens, tokens), 0) == iota((tokens, tokens), 1))
     high = gates.astype(jnp.bfloat16)
     low = (gates - high.astype(jnp.float32)).astype(jnp.bfloat16)
-    named = dot_t(spread, routes.astype(jnp.float32).astype(jnp.bfloat16))
-    highs, lows = dot_t(spread, high), dot_t(spread, low)
-    expert = iota((lanes, experts), 1).astype(jnp.float32)
-    has = jnp.zeros((lanes, experts), jnp.float32)
+    named = dot_t(same, routes.astype(jnp.float32).astype(jnp.bfloat16))
+    highs, lows = dot_t(same, high), dot_t(same, low)
+    expert = iota((tokens, experts), 1).astype(jnp.float32)
+    has = jnp.zeros((tokens, experts), jnp.float32)
     mix_high, mix_low = has, has
     for k in range(picks):
         match = named[:, k:k + 1] == expert
         has = jnp.where(match, 1.0, has)
         mix_high = jnp.where(match, highs[:, k:k + 1], mix_high)
         mix_low = jnp.where(match, lows[:, k:k + 1], mix_low)
-    dst, src = iota((lanes, lanes), 0), iota((lanes, lanes), 1)
-    before = flags((src < dst) & ((src & -tokens) == (dst & -tokens)))
+    before = flags(iota((tokens, tokens), 1) < iota((tokens, tokens), 0))
     count = dot32(before, has.astype(jnp.bfloat16))
 
     pieces = 4
@@ -66,14 +65,14 @@
     def by_slot(values, n):
         part = slice(n * span, (n + 1) * span)
         return jnp.concatenate(
-            [jnp.where(count[:, part] == float(c), values[:, part], 0.0) for c in range(2)], axis=1
+            [jnp.where(count == float(c), values, 0.0)[:, part] for c in range(2)], axis=1
         ).astype(jnp.bfloat16)
 
     for n in range(pieces):
         out = slice(n * step, (n + 1) * step)
-        sends = dot_t(place, by_slot(has, n))
+        sends = dot_t(place, jnp.concatenate([by_slot(has, n)] * FOLD, axis=0))
         send_ref[out, :] = jnp.where(keep, sends, 0.0).astype(jnp.bfloat16)
-        mixes = jnp.concatenate([by_slot(mix_high, n), by_slot(mix_low, n)], axis=0)
+        mixes = jnp.concatenate([by_slot(mix_high, n)] * FOLD + [by_slot(mix_low, n)] * FOLD, axis=0)
         mix_ref[:, out] = jnp.where(keep_t, dot32(mixes, place_t), 0.0).astype(jnp.bfloat16)
 
 
@@ -107,7 +106,7 @@
     for c in range(COLS):
         span = slice(c * cols, (c + 1) * cols)
         w_copies.append(pltpu.make_async_copy(w_hbm.at[:, span], w_buf.at[:, span], w_sem.at[c]))
-    for copy in small[:3] + k_copies + small[3:] + v_copies + w_copies:
+    for copy in small[:3] + k_copies + small[3:]:
         copy.start()
 
     small[0].wait()
@@ -125,7 +124,7 @@
         left = jnp.where(table[c:c + 1, :] == page, usable[c:c + 1, :], left)
     left = left.astype(jnp.float32)
     owned = jnp.maximum(left[:, :requests], left[:, requests:]) > 0
-    left_ref[...] = jnp.broadcast_to(jnp.max(left, axis=-1, keepdims=True), left_ref.shape)
+    left_ref[:pages, :] = jnp.broadcast_to(jnp.max(left, axis=-1, keepdims=True), (pages, slots))
     apart_ref[...] = jnp.where(owned, 0.0, -jnp.inf)
     owned = flags(owned)
     same = flags(iota((requests, requests), 0) == iota((requests, requests), 1))
@@ -149,6 +148,12 @@
     lane = iota((2 * groups, slots), 1).astype(jnp.float32)
     for b in range(blocks):
         k_copies[b].wait()
+        if b == 0:
+            for copy in v_copies:
+                copy.start()
+        if b == blocks - 1:
+            for copy in w_copies:
+                copy.start()
 
         for p in range(b * BLOCK, (b + 1) * BLOCK, 2):
             keys = jnp.concatenate([k_buf[p], k_buf[p + 1]], axis=1)
@@ -236,7 +241,7 @@
             pltpu.VMEM(routes.shape, jnp.int32),
             pltpu.VMEM(logits.shape, jnp.float32),
             pltpu.VMEM((pages, requests), jnp.float32),
-            pltpu.VMEM((pages, slots), jnp.float32),
+            pltpu.VMEM((pages + groups, slots), jnp.float32),
             tile, tile, tile,
             pltpu.VMEM((requests, groups * dim), jnp.bfloat16),
             pltpu.SemaphoreType.DMA((7,)),

time: 77.1 us -> 76.4 us (level)
  Pallas kernels: 13.9 us -> 13.1 us
where the time goes in v3:
time: 76.4 us; the launch traced here: 76.2 us
  blocking collectives  63 us (82%)
  Pallas kernels  13.1 us (17%)
    all_to_all x1, blocking collectives, local(): arrived = exchange(outgoing.reshape(layout)).reshape(outgoing.shape)  29.8 us
    all_to_all x1, blocking collectives, local(): back = exchange(produced.reshape(layout)).reshape(outgoing.shape)  22.8 us
    all_to_all x1, blocking collectives, local(): lax.all_to_all(partial.reshape(heads, tokens, width), 'kvh', split_axis=0...  10.4 us
    pallas_call x1, Pallas kernels, attend(): pl.pallas_call(attend_kernel, out_shape=(jax.ShapeDtypeStruct((requests,...  8.39 us
    pallas_call x1, Pallas kernels, expert(): pl.pallas_call(expert_kernel, out_shape=jax.ShapeDtypeStruct(arrived.shap...  3.26 us

profile of v3, /device:TPU:1, one launch (start us, length us, event | category | flops | bytes accessed | tf_op | source)
XLA Modules:
  0.0 76.2 jit_solution(7973360706820481791)
XLA Ops:
  0.0 0.0 copy-start.1
  0.0 0.0 copy-start.2
  0.0 8.4 %attend.1 = (bf16[64,2048]{1,0:T(8,128)(2,1)S(1)}, bf16[1024,64]{1,0:T(8,128)(2,1)S(1)}, bf16[128,1024]{1,0:T(8,128)(2,1)S(1)}, bf16[16,2048]{1,0:T(8,128)(2,1)S(1)}, bf16[16,128]{1,0:T(8,128)(2,1)S(1)}) custom-call(s32[1,64]{1,0:T(1,128)} %bitcast.31, s32[32,64]{1,0:T(8,128)} %bitcast.27, bf16[64,8,128]{2,1,0:T(8,128)(2,1)} %bitcast.26, ...), custom_call_target="tpu_custom_call" | custom-call | tf_op jit(solution)/shard_map/attend/pallas_call | solution.py:223
  8.4 0.0 copy-start
  8.4 10.4 %all_to_all.15.part_ref = bf16[4,16,2048]{2,1,0:T(8,128)(2,1)S(1)} all-to-all(bf16[4,16,2048]{2,1,0:T(8,128)(2,1)S(1)} %bitcast.23), channel_id=1, replica_groups=mesh['req'=32,'kvh'=4] {'kvh'}, dimensions={0} | all-to-all | bytes 524288 | tf_op jit(solution)/shard_map/all_to_all | solution.py:377
  18.9 0.6 dispatch.1
  19.4 29.8 %all_to_all.16 = bf16[128,8,512]{2,1,0:T(8,128)(2,1)S(1)} all-to-all(bf16[128,8,512]{2,1,0:T(8,128)(2,1)S(1)} %bitcast.22), channel_id=1, replica_groups=mesh['req'=32,'kvh'=4] {'req','kvh'}, dimensions={0} | all-to-all | bytes 2097152 | tf_op jit(solution)/shard_map/all_to_all | solution.py:383
  49.2 0.0 copy-done.1
  49.2 0.0 copy-done.2
  49.2 0.0 copy-done
  49.2 3.3 %expert.1 = bf16[1024,512]{1,0:T(8,128)(2,1)S(1)} custom-call(bf16[1024,512]{1,0:T(8,128)(2,1)S(1)} %bitcast.17, bf16[2048,768]{1,0:T(8,128)(2,1)S(1)} %bitcast.19, bf16[2048,768]{1,0:T(8,128)(2,1)S(1)} %bitcast.20, bf16[768,2048]{1,0:T(8,128)(2,1)S(1)} %bitcast.21), custom_call_target="tpu_custom_call" | custom-call | tf_op jit(solution)/shard_map/expert/pallas_call | solution.py:320
  52.4 22.8 %all_to_all.17 = bf16[128,8,512]{2,1,0:T(8,128)(2,1)S(1)} all-to-all(bf16[128,8,512]{2,1,0:T(8,128)(2,1)S(1)} %bitcast.18), channel_id=1, replica_groups=mesh['req'=32,'kvh'=4] {'req','kvh'}, dimensions={0} | all-to-all | bytes 2097152 | tf_op jit(solution)/shard_map/all_to_all | solution.py:385
  75.3 0.9 %combine.1 = bf16[16,2048]{1,0:T(8,128)(2,1)} custom-call(bf16[1024,512]{1,0:T(8,128)(2,1)S(1)} %bitcast.16, f32[16,2048]{1,0:T(8,128)S(1)} %get-tuple-element.17.stream_ref, bf16[128,1024]{1,0:T(8,128)(2,1)S(1)} %get-tuple-element.18.mix_ref), custom_call_target="tpu_custom_call" | custom-call | tf_op jit(solution)/shard_map/combine/pallas_call | solution.py:345
Async XLA Ops:
  0.0 49.2 %copy-start.1 = (bf16[1,2048,768]{2,1,0:T(8,128)(2,1)S(1)}, bf16[1,2048,768]{2,1,0:T(8,128)(2,1)}, u32[]{:S(2)}) copy-start(bf16[1,2048,768]{2,1,0:T(8,128)(2,1)} %param.24) | copy-start | bytes 9437188
  0.0 49.2 %copy-start.2 = (bf16[1,768,2048]{2,1,0:T(8,128)(2,1)S(1)}, bf16[1,768,2048]{2,1,0:T(8,128)(2,1)}, u32[]{:S(2)}) copy-start(bf16[1,768,2048]{2,1,0:T(8,128)(2,1)} %param.25) | copy-start | bytes 9437188
  8.4 40.8 %copy-start = (bf16[1,2048,768]{2,1,0:T(8,128)(2,1)S(1)}, bf16[1,2048,768]{2,1,0:T(8,128)(2,1)}, u32[]{:S(2)}) copy-start(bf16[1,2048,768]{2,1,0:T(8,128)(2,1)} %param.23) | copy-start | bytes 9437188
